TPU v7x, 256 devices: a whole 4x4x8 slice. The times are simulated.
256 devices in a mesh: rows: 8 (over z_hi, core), cols: 32 (over x, y, z_lo).
Axes of the slice: x: 4, y: 4, z: 8 (z_hi: 4, z_lo: 2; z = z_hi * 2 + z_lo), core: 2. Of those that a mesh axis runs over, the one named last changes fastest.
Arguments:
- covariance: float32 [16384, 16384], P('rows', 'cols'), may hold values from -0.5 to 9.5, as said below
- prior_concentration: float32 [16384], replicated, may hold values from -6 to 6
- east_wind: float32 [64, 256], replicated, may hold values from -0.35 to 0.35
- north_wind: float32 [64, 256], replicated, may hold values from -0.35 to 0.35
- diffusivity: float32 [64, 256], replicated, may hold values from 0.02 to 0.07
- sensor_cell_position: int32 [128, 16], replicated, may hold values from 0 to 16383, as said below
- sensor_cell_share: float32 [128, 16], replicated, may hold values from 0.1 to 0.4
- measurement_readings: float32 [128], replicated, may hold values from -6 to 6
- obs_variance: float32 [128], replicated, may hold values from 0.2 to 2
Outputs:
- cov_analysis: float32 [16384, 16384], P('rows', 'cols')
- corrected_concentration: float32 [16384], P('rows')
Inputs may be any that keep to these rules, and one draw needn't show every extreme that they name: `covariance`: symmetric and positive definite. `sensor_cell_position`: the 16 indices of an observation are the cells of a 4 x 4 patch of neighbouring latitudes and longitudes (longitudes wrap), index = latitude * 256 + longitude.
All inputs are finite; a program needn't handle non-finite values.
Results may differ from a plain program's by a relative error of at most 0.00011.
Values sent between devices are 32-bit elements; how exact they have to be, the bound alone decides.
No kernel may reach another device: no remote copies, remote signals or barrier semaphores. Data moves between devices by JAX's collectives and lax.ppermute only.
A program may use at most 128 MiB of HBM per device.

v0:
```python
import functools

import jax
import jax.numpy as jnp
from jax import lax
from jax.experimental import pallas as pl
from jax.experimental.pallas import tpu as pltpu
from jax.sharding import PartitionSpec as P

HI = lax.Precision.HIGHEST
LON = 256
OBS = 128
SMALL = pl.CostEstimate(flops=1, bytes_accessed=1, transcendentals=0)


def after(value, *others):
    return lax.optimization_barrier((value, *others))[0]


def coefficients(east_wind, north_wind, diffusivity):
    western = jnp.maximum(east_wind, 0.0) + diffusivity
    eastern = jnp.maximum(-east_wind, 0.0) + diffusivity
    southern = jnp.maximum(north_wind, 0.0) + diffusivity
    northern = jnp.maximum(-north_wind, 0.0) + diffusivity
    middle = 1.0 - (western + eastern + southern + northern)
    return (middle, western, eastern, southern, northern)


def row_kernel(groups, n_in, outs, *refs):
    coef = refs[n_in]
    out_refs = refs[n_in + 1 : n_in + 1 + len(outs)]
    wide, mid = refs[n_in + 1 + len(outs) :]

    @pl.when(pl.program_id(0) == 0)
    def _():
        at = 0
        for _, off, n in groups:
            for j in range(n + 2):
                for k in range(5):
                    column = coef[(off + j) * LON : (off + j + 1) * LON, k : k + 1]
                    wide[k, at + j] = jnp.broadcast_to(column, (LON, 128))
            at += n + 2

    def step(j, here, south, north):
        west = pltpu.roll(here, 1, axis=0)
        east = pltpu.roll(here, LON - 1, axis=0)
        return (
            wide[0, j] * here
            + wide[1, j] * west
            + wide[2, j] * east
            + wide[3, j] * south
            + wide[4, j] * north
        )

    places = [(ref, i) for ref, count in zip(out_refs, outs) for i in range(count)]
    at = 0
    for sources, _, n in groups:

        def source(i):
            which, lat = sources[i]
            return refs[which][lat * LON : (lat + 1) * LON, :]

        for j in range(n + 2):
            mid[j] = step(at + j, source(j + 1), source(j), source(j + 2))
        for j in range(1, n + 1):
            ref, i = places.pop(0)
            ref[i * LON : (i + 1) * LON, :] = step(at + j, mid[j], mid[j - 1], mid[j + 1])
        at += n + 2


def row_steps(arrays, coef, groups, outs):
    cols = arrays[0].shape[1]
    total = sum(n + 2 for _, _, n in groups)
    return pl.pallas_call(
        functools.partial(row_kernel, groups, len(arrays), outs),
        grid=(cols // 128,),
        in_specs=[pl.BlockSpec((a.shape[0], 128), lambda i: (0, i)) for a in arrays]
        + [pl.BlockSpec(coef.shape, lambda i: (0, 0))],
        out_specs=[pl.BlockSpec((count * LON, 128), lambda i: (0, i)) for count in outs],
        out_shape=[jax.ShapeDtypeStruct((count * LON, cols), jnp.float32) for count in outs],
        scratch_shapes=[
            pltpu.VMEM((5, total, LON, 128), jnp.float32),
            pltpu.VMEM((max(n for _, _, n in groups) + 2, LON, 128), jnp.float32),
        ],
        compiler_params=pltpu.CompilerParams(vmem_limit_bytes=60 << 20),
        cost_estimate=SMALL,
        name="row_step",
    )(*arrays, coef)


def inner_step(own, coef):
    return row_steps([own], coef, [([(0, i) for i in range(8)], 2, 4)], (2, 2))


def edge_step(below, own, above, coef):
    first = [(0, 0), (0, 1)] + [(1, i) for i in range(4)]
    second = [(1, i) for i in range(4, 8)] + [(2, 0), (2, 1)]
    return row_steps([below, own, above], coef, [(first, 0, 2), (second, 6, 2)], (2, 2))


TILE = 16


def column_kernel(mode, block, flag, *refs):
    blocks, coef, out, wide = refs[:-3], refs[-3], refs[-2], refs[-1]

    @pl.when(pl.program_id(0) == 0)
    def _():
        for i in range(20):
            wide[i] = jnp.broadcast_to(coef[i : i + 1, :], (8, LON))

    low_bit = flag[0]
    zero = jnp.zeros((TILE, LON), jnp.float32)

    def times(i, x):
        return x if x is zero else jnp.concatenate([wide[i]] * (TILE // 8), 0) * x

    def step(j, here, south, north):
        if here is zero:
            terms = []
        else:
            terms = [
                times(5 * j, here),
                times(5 * j + 1, pltpu.roll(here, 1, axis=1)),
                times(5 * j + 2, pltpu.roll(here, LON - 1, axis=1)),
            ]
        terms += [times(5 * j + 3, south)] if south is not zero else []
        terms += [times(5 * j + 4, north)] if north is not zero else []
        return functools.reduce(lambda x, y: x + y, terms)

    def tile(t, carry):
        at = pl.ds(pl.multiple_of(t * TILE, TILE), TILE)
        f = [zero] * 6
        if mode != "others":
            f[2], f[3] = blocks[0][at, :LON], blocks[0][at, LON:]
        if mode != "own":
            near, far = blocks[-2][at, :], blocks[-1][at, :]
            below = jnp.where(low_bit == 0, far, near)
            above = jnp.where(low_bit == 0, near, far)
            f[0], f[1], f[4], f[5] = below[:, :LON], below[:, LON:], above[:, :LON], above[:, LON:]
        g = [step(j, f[j + 1], f[j], f[j + 2]) for j in range(4)]
        out[at, :LON] = step(1, g[1], g[0], g[2])
        out[at, LON:] = step(2, g[2], g[1], g[3])
        return carry

    lax.fori_loop(0, block // TILE, tile, 0, unroll=4)


def column_step(mode, flag, blocks, coef):
    rows, block = blocks[0].shape[0], 128
    spec = pl.BlockSpec((block, 2 * LON), lambda i: (i, 0))
    return pl.pallas_call(
        functools.partial(column_kernel, mode, block),
        grid=(rows // block,),
        in_specs=[pl.BlockSpec(memory_space=pltpu.SMEM)]
        + [spec] * len(blocks)
        + [pl.BlockSpec(coef.shape, lambda i: (0, 0))],
        out_specs=spec,
        out_shape=jax.ShapeDtypeStruct((rows, 2 * LON), jnp.float32),
        scratch_shapes=[pltpu.VMEM((20, 8, LON), jnp.float32)],
        compiler_params=pltpu.CompilerParams(vmem_limit_bytes=40 << 20),
        cost_estimate=SMALL,
        name="column_step_" + mode,
    )(flag, *blocks, coef)


def correct_kernel(n, *refs):
    left, right, out = refs[n], refs[n + 1], refs[-1]
    forecast = refs[0][...] if n == 1 else refs[0][...] + refs[1][...]
    out[...] = forecast - jnp.dot(
        left[...], right[...], precision=HI, preferred_element_type=jnp.float32
    )


def correct(terms, left, right, first_lat, into):
    rows, n = terms[0].shape[0], len(terms)
    aliased = [] if into is None else [into]
    return pl.pallas_call(
        functools.partial(correct_kernel, n),
        grid=(rows // LON,),
        in_specs=[pl.BlockSpec((LON, 2 * LON), lambda i: (i, 0))] * n
        + [
            pl.BlockSpec((LON, OBS), lambda i: (first_lat + i, 0)),
            pl.BlockSpec(right.shape, lambda i: (0, 0)),
        ]
        + [pl.BlockSpec(memory_space=pl.ANY)] * len(aliased),
        out_specs=pl.BlockSpec((LON, 2 * LON), lambda i: (first_lat + i, 0)),
        out_shape=jax.ShapeDtypeStruct((8 * LON, 2 * LON), jnp.float32),
        input_output_aliases={n + 2: 0} if aliased else {},
        compiler_params=pltpu.CompilerParams(vmem_limit_bytes=40 << 20),
        cost_estimate=SMALL,
        name="correct",
    )(*terms, left, right, *aliased)


def adjoint_kernel(n, start, position, share, coef, out, first, second):
    lane = lax.broadcasted_iota(jnp.int32, (OBS, LON), 1)
    for i in range(n + 4):
        base = start[0] + i * LON
        total = jnp.zeros((OBS, LON), jnp.float32)
        for f in range(position.shape[1]):
            hit = (position[:, f : f + 1] - base) == lane
            total = total + jnp.where(hit, share[:, f : f + 1], 0.0)
        first[i] = total

    def adjoint(field, i):
        def c(k, j):
            return coef[k * (n + 4) + j : k * (n + 4) + j + 1, :]

        here = field[i]
        return (
            c(0, i) * here
            + pltpu.roll(c(1, i) * here, LON - 1, axis=1)
            + pltpu.roll(c(2, i) * here, 1, axis=1)
            + c(3, i + 1) * field[i + 1]
            + c(4, i - 1) * field[i - 1]
        )

    for i in range(1, n + 3):
        second[i] = adjoint(first, i)
    for i in range(2, n + 2):
        out[:, (i - 2) * LON : (i - 1) * LON] = adjoint(second, i)


def adjoint_footprints(start, position, share, coef, n):
    vmem = pl.BlockSpec(memory_space=pltpu.VMEM)
    return pl.pallas_call(
        functools.partial(adjoint_kernel, n),
        in_specs=[pl.BlockSpec(memory_space=pltpu.SMEM), vmem, vmem, vmem],
        out_specs=vmem,
        out_shape=jax.ShapeDtypeStruct((OBS, n * LON), jnp.float32),
        scratch_shapes=[pltpu.VMEM((n + 4, OBS, LON), jnp.float32)] * 2,
        compiler_params=pltpu.CompilerParams(vmem_limit_bytes=40 << 20),
        cost_estimate=SMALL,
        name="adjoint_footprints",
    )(start, position, share, coef)


def footprints_kernel(lats, start, position, share, out):
    lane = lax.broadcasted_iota(jnp.int32, (OBS, LON), 1)
    for i in range(lats):
        base = start[0] + i * LON
        total = jnp.zeros((OBS, LON), jnp.float32)
        for f in range(position.shape[1]):
            hit = (position[:, f : f + 1] - base) == lane
            total = total + jnp.where(hit, share[:, f : f + 1], 0.0)
        out[:, i * LON : (i + 1) * LON] = total


def footprints(start, position, share, lats):
    vmem = pl.BlockSpec(memory_space=pltpu.VMEM)
    return pl.pallas_call(
        functools.partial(footprints_kernel, lats),
        in_specs=[pl.BlockSpec(memory_space=pltpu.SMEM), vmem, vmem],
        out_specs=vmem,
        out_shape=jax.ShapeDtypeStruct((OBS, lats * LON), jnp.float32),
        compiler_params=pltpu.CompilerParams(vmem_limit_bytes=40 << 20),
        cost_estimate=SMALL,
        name="footprints",
    )(start, position, share)


def dot_rows(a, b):
    return lax.dot_general(
        a, b, (((1,), (1,)), ((), ())), precision=HI, preferred_element_type=jnp.float32
    )


def project_kernel(*refs):
    blocks, g, v_out = refs[:-2], refs[-2], refs[-1]
    at = 0
    for ref in blocks:
        for i in range(0, ref.shape[0], LON):
            v_out[at : at + LON, :] = dot_rows(ref[i : i + LON, :], g[...])
            at += LON


def project(blocks, g):
    vmem = pl.BlockSpec(memory_space=pltpu.VMEM)
    rows = sum(a.shape[0] for a in blocks)
    return pl.pallas_call(
        project_kernel,
        in_specs=[vmem] * (len(blocks) + 1),
        out_specs=vmem,
        out_shape=jax.ShapeDtypeStruct((rows, OBS), jnp.float32),
        compiler_params=pltpu.CompilerParams(vmem_limit_bytes=40 << 20),
        cost_estimate=SMALL,
        name="project",
    )(*blocks, g)


def inverse_kernel(gram, variance, out):
    row = lax.broadcasted_iota(jnp.int32, (OBS, OBS), 0)
    lane = lax.broadcasted_iota(jnp.int32, (OBS, OBS), 1)
    a = gram[...] + jnp.where(row == lane, variance[...], 0.0)
    at = lax.broadcasted_iota(jnp.int32, (1, OBS), 1)
    for k in range(OBS):
        column = jnp.broadcast_to(a[:, k : k + 1], (OBS, OBS))
        pivot = 1.0 / column[k : k + 1, :]
        line = jnp.where(at == k, 1.0, a[k : k + 1, :]) * pivot
        a = jnp.where(lane == k, 0.0, a) - column * line
        a = jnp.where(row == k, line, a)
    out[...] = a


def inverse(gram, variance):
    vmem = pl.BlockSpec(memory_space=pltpu.VMEM)
    return pl.pallas_call(
        inverse_kernel,
        in_specs=[vmem, vmem],
        out_specs=vmem,
        out_shape=jax.ShapeDtypeStruct((OBS, OBS), jnp.float32),
        cost_estimate=SMALL,
        name="inverse",
    )(gram, variance)


def shards(
    covariance,
    prior_concentration,
    east_wind,
    north_wind,
    diffusivity,
    sensor_cell_position,
    sensor_cell_share,
    measurement_readings,
    obs_variance,
):
    rows_n, cols_n = lax.axis_size("rows"), lax.axis_size("cols")
    r, c = lax.axis_index("rows"), lax.axis_index("cols")
    up = [(i, i + 1) for i in range(rows_n - 1)]
    down = [(j, i) for i, j in up]
    swap = [(i, i ^ 1) for i in range(cols_n)]
    onward = [(i, i + 2) for i in range(0, cols_n - 2, 2)]
    onward += [(i, i - 2) for i in range(3, cols_n, 2)]
    planes = [[2 * i + k for i in range(cols_n // 2)] for k in range(2)]

    from_below = lax.ppermute(covariance[6 * LON :], "rows", up)
    from_above = lax.ppermute(covariance[: 2 * LON], "rows", down)

    coefs = coefficients(east_wind, north_wind, diffusivity)
    padded = jnp.pad(jnp.stack(coefs), ((0, 0), (2, 2), (0, 0)))
    row_band = lax.dynamic_slice_in_dim(padded, 8 * r, 12, 1)
    col_band = lax.dynamic_slice_in_dim(padded, 2 * c, 6, 1)
    down_coef = jnp.pad(row_band[:, 1:11].reshape(5, 10 * LON).T, ((0, 0), (0, 3)))
    across_coef = jnp.pad(col_band[:, 1:5].transpose(1, 0, 2).reshape(20, LON), ((0, 4), (0, 0)))

    inner = inner_step(covariance, down_coef)

    flag = (c % 2)[None]

    back = [(i, i + 2) for i in range(1, cols_n - 2, 2)]
    back += [(i, i - 2) for i in range(2, cols_n, 2)]
    other_band = lax.dynamic_slice_in_dim(padded, 2 * (c ^ 1), 6, 1)
    other_coef = jnp.pad(
        other_band[:, 1:5].transpose(1, 0, 2).reshape(20, LON), ((0, 4), (0, 0))
    )
    a1, b1 = inner
    got_a1 = lax.ppermute(a1, "cols", swap)
    raw_b1 = lax.ppermute(b1, "cols", back)

    g_col = adjoint_footprints(
        ((2 * c - 2) * LON)[None],
        sensor_cell_position,
        sensor_cell_share,
        col_band.reshape(30, LON),
        2,
    )
    v_inner = project([a1, b1], g_col)

    a2, b2 = edge_step(from_below, covariance, from_above, down_coef)
    got_a2 = lax.ppermute(a2, "cols", swap)
    raw_b2 = lax.ppermute(b2, "cols", back)
    v_outer = project([a2, b2], g_col)
    v_part = jnp.concatenate([v_outer[: 2 * LON], v_inner, v_outer[2 * LON :]])

    field = prior_concentration.reshape(-1, LON)
    for _ in range(2):
        ext = jnp.pad(field, ((1, 1), (0, 0)))
        field = (
            coefs[0] * field
            + coefs[1] * jnp.roll(field, 1, axis=1)
            + coefs[2] * jnp.roll(field, -1, axis=1)
            + coefs[3] * ext[:-2]
            + coefs[4] * ext[2:]
        )
    flat = sensor_cell_position.reshape(-1)
    lat_hot = (flat[:, None] // LON == jnp.arange(field.shape[0])[None, :]).astype(jnp.float32)
    lines = jnp.dot(lat_hot, field, precision=HI)
    lon_hot = flat[:, None] % LON == jnp.arange(LON)[None, :]
    picked = jnp.sum(jnp.where(lon_hot, lines, 0.0), axis=1).reshape(sensor_cell_position.shape)
    innovation = measurement_readings - jnp.sum(sensor_cell_share * picked, axis=1)

    arrived = lax.all_to_all(
        v_part.reshape(16, 128, OBS), "cols", 0, 0, axis_index_groups=planes, tiled=True
    )
    far_a1 = lax.ppermute(got_a1, "cols", onward)
    part_b1 = column_step("others", 1 - flag, [b1, raw_b1], other_coef)
    part_b2 = column_step("others", 1 - flag, [b2, raw_b2], other_coef)
    piece = after(arrived, part_b1, got_a1).sum(axis=0)
    other = lax.ppermute(piece, "cols", swap)
    sum_b1 = lax.ppermute(after(part_b1, piece), "cols", swap)
    h_row = footprints((8 * r * LON)[None], sensor_cell_position, sensor_cell_share, 8)
    whole = lax.all_to_all(
        jnp.broadcast_to(after(piece + other, got_a2)[None], (16, 128, OBS)),
        "cols",
        0,
        0,
        axis_index_groups=planes,
        tiled=True,
    )
    v_row = after(whole, h_row, part_b2, sum_b1, far_a1, innovation).reshape(8 * LON, OBS)
    far_a2 = lax.ppermute(after(got_a2, v_row), "cols", onward)

    gram = jnp.dot(h_row, v_row, precision=HI)
    v_col = lax.dynamic_slice_in_dim(v_row, (c % 4) * 2 * LON, 2 * LON, 0)
    v_col = jnp.where(r == c // 4, v_col, 0.0)
    both = jnp.concatenate([gram, v_col])
    both = both + lax.ppermute(both, "rows", [(i, i ^ 1) for i in range(rows_n)])
    gram, v_col = both[:OBS], both[OBS:]
    gram = gram + lax.ppermute(gram, "rows", [(i, i ^ 2) for i in range(rows_n)])
    gram = gram + lax.ppermute(gram, "rows", [(i, i ^ 4) for i in range(rows_n)])
    mine = jnp.where(r // 2 == c // 8, v_col, 0.0)
    v_col = mine
    for d in (1, 2, 3):
        hop = []
        for col in range(cols_n):
            z = col // 8
            for core in range(2):
                src, dst = 2 * z + core, 2 * ((z + d) % 4) + core
                hop.append((src * cols_n + col, dst * cols_n + col))
        v_col = v_col + lax.ppermute(mine, ("rows", "cols"), hop)
    own_b1 = column_step("own", flag, [after(b1, v_row)], across_coef)
    own_b2 = column_step("own", flag, [after(b2, v_row)], across_coef)
    f_a1 = column_step("all", flag, [after(a1, v_row), got_a1, far_a1], across_coef)
    gram, v_col, own_b1, own_b2, f_a1, _ = lax.optimization_barrier(
        (gram, v_col, own_b1, own_b2, f_a1, far_a2)
    )
    sum_b2 = lax.ppermute(after(part_b2, gram), "cols", swap)

    weights = inverse(gram, obs_variance[None])
    f_a2 = column_step("all", flag, [a2, got_a2, far_a2], across_coef)
    right = dot_rows(weights, v_col)
    solved = jnp.sum(weights * innovation[None], axis=1)
    mean_band = lax.dynamic_slice_in_dim(field, 8 * r, 8, 0).reshape(-1)
    corrected = mean_band + jnp.sum(v_row * solved[None], axis=1)

    out = None
    for first_lat, terms in (
        (4, [own_b1, sum_b1]),
        (2, [f_a1]),
        (6, [own_b2, sum_b2]),
        (0, [f_a2]),
    ):
        out = correct(terms, v_row, right, first_lat, out)
    return (out, corrected)


def solution(mesh):
    return jax.shard_map(
        shards,
        mesh=mesh,
        in_specs=(P("rows", "cols"), P(), P(), P(), P(), P(), P(), P(), P()),
        out_specs=(P("rows", "cols"), P("rows")),
        check_vma=False,
    )
```

profile of v0, /device:TPU:34, one launch (start us, length us, event | category | flops | bytes accessed | tf_op | source)
XLA Modules:
  0.0 195.8 jit_solution(7040095016785962311)
XLA Ops:
  0.7 3.2 %fusion.19 = (f32[512,512]{1,0:T(8,128)}, f32[512,512]{1,0:T(8,128)}) fusion(f32[2048,512]{1,0:T(8,128)} %refs_0_.1), kind=kLoop, calls=%fused_computation.61 | loop fusion | bytes 4194304 | tf_op jit(solution)/shard_map/slice | solution.py:339
  5.1 4.0 %collective-permute-start = (f32[512,512]{1,0:T(8,128)}, f32[512,512]{1,0:T(8,128)}, u32[]{:S(2)}, u32[]{:S(2)}) collective-permute-start(f32[512,512]{1,0:T(8,128)} %get-tuple-element.44), channel_id=1, source_target_pairs={{0,32},{32,64},{64,96},{96,128},{128,160},{160,192},{192,224},{1,3... | collective-permute-start | bytes 3145736 | tf_op jit(solution)/shard_map/ppermute | solution.py:338
  11.2 6.7 %row_step.3 = (f32[512,512]{1,0:T(8,128)}, f32[512,512]{1,0:T(8,128)}) custom-call(f32[2048,512]{1,0:T(8,128)} %refs_0_.1, f32[2560,8]{1,0:T(8,128)} %pad.23.refs_3_.refs_1_), custom_call_target="tpu_custom_call" | custom-call | flops 1 | bytes 1 | tf_op jit(solution)/shard_map/row_step/pallas_call | solution.py:74
  18.3 4.4 %adjoint_footprints.1.refs_2_ = f32[128,512]{1,0:T(8,128)S(1)} custom-call(s32[1]{0:T(128)} %bitcast.8.start, s32[128,16]{1,0:T(8,128)S(1)} %copy.22.position, f32[128,16]{1,0:T(8,128)S(1)} %copy.23.share, f32[30,256]{1,0:T(8,128)S(1)} %reshape.128.coef), custom_call_target="tpu_custom_call" | custom-call | flops 1 | bytes 1 | tf_op jit(solution)/shard_map/adjoint_footprints/pallas_call | solution.py:227
  22.7 3.7 %collective-permute-start.3 = (f32[512,512]{1,0:T(8,128)}, f32[512,512]{1,0:T(8,128)}, u32[]{:S(2)}, u32[]{:S(2)}) collective-permute-start(f32[512,512]{1,0:T(8,128)} %get-tuple-element.29.refs_1_.refs_0_), channel_id=1, source_target_pairs={{1,3},{3,5},{5,7},{7,9},{9,11},{11,13},{13,15},{15,17},{17,19},{19... | collective-permute-start | bytes 3145736 | tf_op jit(solution)/shard_map/ppermute | solution.py:360
  30.7 8.2 %row_step.2 = (f32[512,512]{1,0:T(8,128)}, f32[512,512]{1,0:T(8,128)}) custom-call(f32[512,512]{1,0:T(8,128)} %collective-permute-done.refs_0_, f32[2048,512]{1,0:T(8,128)} %refs_0_.1, f32[512,512]{1,0:T(8,128)} %collective-permute-done.1.refs_2_, f32[2560,8]{1,0:T(8,128)} %pad.23.refs_3_.refs_1_), custom_call_target="tpu_custom_call" | custom-call | flops 1 | bytes 1 | tf_op jit(solution)/shard_map/row_step/pallas_call | solution.py:74
  41.3 1.8 project.2
  44.3 7.3 %all-to-all-start = ((f32[16,128,128]{2,1,0:T(8,128)}), f32[16,128,128]{2,1,0:T(8,128)}, u32[]{:S(2)}, u32[]{:S(2)}) async-start(f32[16,128,128]{2,1,0:T(8,128)} %bitcast.9), calls=%async_computation | async-start | bytes 2097152 | tf_op jit(solution)/shard_map/all_to_all | solution.py:394
  54.1 3.3 %column_step_others.2 = f32[512,512]{1,0:T(8,128)S(1)} custom-call(s32[1]{0:T(128)S(6)} %sub.35.flag, f32[512,512]{1,0:T(8,128)S(1)} %copy-done.1, f32[512,512]{1,0:T(8,128)} %collective-permute-done.3.refs_1_, f32[24,256]{1,0:T(8,128)S(1)} %pad.24.refs_2_), custom_call_target="tpu_custom_call" | custom-call | flops 1 | bytes 1 | tf_op jit(solution)/shard_map/column_step_others/pallas_call | solution.py:152
  58.4 7.4 %all-to-all-done = f32[16,128,128]{2,1,0:T(8,128)} async-done(((f32[16,128,128]{2,1,0:T(8,128)}), f32[16,128,128]{2,1,0:T(8,128)}, u32[]{:S(2)}, u32[]{:S(2)}) %all-to-all-start) | async-done | bytes 1048608 | tf_op jit(solution)/shard_map/all_to_all | solution.py:394
  65.8 1.9 reduce_sum.47
  67.7 4.5 %collective-permute-start.5 = (f32[128,128]{1,0:T(8,128)}, f32[128,128]{1,0:T(8,128)}, u32[]{:S(2)}, u32[]{:S(2)}) collective-permute-start(f32[128,128]{1,0:T(8,128)} %reduce_sum.47), channel_id=1, source_target_pairs={{0,1},{1,0},{2,3},{3,2},{4,5},{5,4},{6,7},{7,6},{8,9},{9,8},{10,11... | collective-permute-start | bytes 196616 | tf_op jit(solution)/shard_map/ppermute | solution.py:401
  72.2 2.5 %collective-permute-start.6 = (f32[512,512]{1,0:T(8,128)S(1)}, f32[512,512]{1,0:T(8,128)}, u32[]{:S(2)}, u32[]{:S(2)}) collective-permute-start(f32[512,512]{1,0:T(8,128)S(1)} %copy-done.3), channel_id=1, source_target_pairs={{1,3},{3,5},{5,7},{7,9},{9,11},{11,13},{13,15},{15,17},{17,19},{19... | collective-permute-start | bytes 3145736 | tf_op jit(solution)/shard_map/ppermute | solution.py:373
  74.7 5.5 %collective-permute-start.8 = (f32[512,512]{1,0:T(8,128)}, f32[512,512]{1,0:T(8,128)}, u32[]{:S(2)}, u32[]{:S(2)}) collective-permute-start(f32[512,512]{1,0:T(8,128)} %collective-permute-done.4.refs_1_), channel_id=1, source_target_pairs={{0,2},{2,4},{4,6},{6,8},{8,10},{10,12},{12,14},{14,16},{16,18},{18... | collective-permute-start | bytes 3145736 | tf_op jit(solution)/shard_map/ppermute | solution.py:397
  82.3 5.8 %all-to-all-start.1 = ((f32[16,128,128]{2,1,0:T(8,128)}), f32[16,128,128]{2,1,0:T(8,128)S(1)}, u32[]{:S(2)}, u32[]{:S(2)}) async-start(f32[16,128,128]{2,1,0:T(8,128)} %broadcast_in_dim.33), calls=%async_computation.1 | async-start | bytes 2097152 | tf_op jit(solution)/shard_map/all_to_all | solution.py:404
  88.1 5.2 %footprints.1 = f32[128,2048]{1,0:T(8,128)S(1)} custom-call(s32[1]{0:T(128)} %bitcast.11.start, s32[128,16]{1,0:T(8,128)S(1)} %copy.22.position, f32[128,16]{1,0:T(8,128)S(1)} %copy.23.share), custom_call_target="tpu_custom_call" | custom-call | flops 1 | bytes 1 | tf_op jit(solution)/shard_map/footprints/pallas_call | solution.py:252
  97.9 11.5 %collective-permute-done.6.refs_1_ = f32[512,512]{1,0:T(8,128)} collective-permute-done((f32[512,512]{1,0:T(8,128)S(1)}, f32[512,512]{1,0:T(8,128)}, u32[]{:S(2)}, u32[]{:S(2)}) %collective-permute-start.6) | collective-permute-done | bytes 1048608 | tf_op jit(solution)/shard_map/ppermute | solution.py:373
  109.4 4.2 %column_step_others.3 = f32[512,512]{1,0:T(8,128)} custom-call(s32[1]{0:T(128)S(6)} %sub.35.flag, f32[512,512]{1,0:T(8,128)S(1)} %copy-done.3, f32[512,512]{1,0:T(8,128)} %collective-permute-done.6.refs_1_, f32[24,256]{1,0:T(8,128)S(1)} %pad.24.refs_2_), custom_call_target="tpu_custom_call" | custom-call | flops 1 | bytes 1 | tf_op jit(solution)/shard_map/column_step_others/pallas_call | solution.py:152
  113.6 7.2 %all-to-all-done.1 = f32[16,128,128]{2,1,0:T(8,128)S(1)} async-done(((f32[16,128,128]{2,1,0:T(8,128)}), f32[16,128,128]{2,1,0:T(8,128)S(1)}, u32[]{:S(2)}, u32[]{:S(2)}) %all-to-all-start.1) | async-done | bytes 1048608 | tf_op jit(solution)/shard_map/all_to_all | solution.py:404
  120.9 2.4 %fusion.25 = f32[128,128]{1,0:T(8,128)S(1)} fusion(f32[128,2048]{1,0:T(8,128)} %copy-done.11, f32[2048,128]{1,0:T(8,128)S(1)} %bitcast.33), kind=kOutput, calls=%fused_computation.67 | convolution fusion | flops 402653184 | bytes 2162688 | tf_op jit(solution)/shard_map/dot_general | solution.py:415
  124.1 6.4 %collective-permute-start.9 = (f32[512,512]{1,0:T(8,128)}, f32[512,512]{1,0:T(8,128)}, u32[]{:S(2)}, u32[]{:S(2)}) collective-permute-start(f32[512,512]{1,0:T(8,128)} %collective-permute-done.2.refs_1_), channel_id=1, source_target_pairs={{0,2},{2,4},{4,6},{6,8},{8,10},{10,12},{12,14},{14,16},{16,18},{18... | collective-permute-start | bytes 3145736 | tf_op jit(solution)/shard_map/ppermute | solution.py:413
  131.6 3.3 %collective-permute-start.11 = (f32[128,128]{1,0:T(8,128)S(1)}, f32[128,128]{1,0:T(8,128)S(1)}, u32[]{:S(2)}, u32[]{:S(2)}) collective-permute-start(f32[128,128]{1,0:T(8,128)S(1)} %slice.98), channel_id=1, source_target_pairs={{0,64},{32,96},{64,0},{96,32},{128,192},{160,224},{192,128},{224,1... | collective-permute-start | bytes 196616 | tf_op jit(solution)/shard_map/ppermute | solution.py:421
  142.5 2.3 %column_step_own.3.refs_0_ = f32[512,512]{1,0:T(8,128)S(1)} custom-call(s32[1]{0:T(128)} %bitcast.flag, f32[512,512]{1,0:T(8,128)S(1)} %copy-done.3, f32[24,256]{1,0:T(8,128)S(1)} %pad.27.refs_3_.refs_1_), custom_call_target="tpu_custom_call" | custom-call | flops 1 | bytes 1 | tf_op jit(solution)/shard_map/column_step_own/pallas_call | solution.py:152
  145.8 2.3 %column_step_own.2.refs_0_ = f32[512,512]{1,0:T(8,128)S(1)} custom-call(s32[1]{0:T(128)} %bitcast.flag, f32[512,512]{1,0:T(8,128)S(1)} %copy-done.1, f32[24,256]{1,0:T(8,128)S(1)} %pad.27.refs_3_.refs_1_), custom_call_target="tpu_custom_call" | custom-call | flops 1 | bytes 1 | tf_op jit(solution)/shard_map/column_step_own/pallas_call | solution.py:152
  149.1 4.3 %column_step_all.3.refs_0_ = f32[512,512]{1,0:T(8,128)S(1)} custom-call(s32[1]{0:T(128)} %bitcast.flag, f32[512,512]{1,0:T(8,128)S(1)} %copy-done.10, f32[512,512]{1,0:T(8,128)} %collective-permute-done.4.refs_1_, f32[512,512]{1,0:T(8,128)} %collective-permute-done.8.refs_2_, f32[24,256]{1,0:T(8,128)S(1)} %pad.27.refs_3_.refs_1_), custom_call_target="tpu_custom_call" | custom-call | flops 1 | bytes 1 | tf_op jit(solution)/shard_map/column_step_all/pallas_call | solution.py:152
  156.9 7.9 %collective-permute-start.16 = (f32[512,512]{1,0:T(8,128)}, f32[512,512]{1,0:T(8,128)}, u32[]{:S(2)}, u32[]{:S(2)}) collective-permute-start(f32[512,512]{1,0:T(8,128)} %column_step_others.3), channel_id=1, source_target_pairs={{0,1},{1,0},{2,3},{3,2},{4,5},{5,4},{6,7},{7,6},{8,9},{9,8},{10,11... | collective-permute-start | bytes 3145736 | tf_op jit(solution)/shard_map/ppermute | solution.py:439
  165.5 12.4 %inverse.1 = f32[128,128]{1,0:T(8,128)} custom-call(f32[128,128]{1,0:T(8,128)} %add.149.gram, f32[1,128]{1,0:T(1,128)} %bitcast.41), custom_call_target="tpu_custom_call" | custom-call | flops 1 | bytes 1 | tf_op jit(solution)/shard_map/inverse/pallas_call | solution.py:308
  180.4 3.0 %correct.4.refs_3_ = f32[2048,512]{1,0:T(8,128)} custom-call(f32[512,512]{1,0:T(8,128)S(1)} %copy-done.13, f32[512,512]{1,0:T(8,128)} %collective-permute-done.7.refs_1_, f32[2048,128]{1,0:T(8,128)S(1)} %bitcast.35, f32[128,512]{1,0:T(8,128)S(1)} %fusion.26.refs_3_.refs_2_), custom_call_target="tpu_custom_call" | custom-call | flops 1 | bytes 1 | tf_op jit(solution)/shard_map/correct/pallas_call | solution.py:178
  183.4 1.9 correct.5.refs_4_
  185.3 4.4 %column_step_all.2.refs_0_ = f32[512,512]{1,0:T(8,128)S(1)} custom-call(s32[1]{0:T(128)} %bitcast.flag, f32[512,512]{1,0:T(8,128)S(1)} %copy-done.8, f32[512,512]{1,0:T(8,128)} %collective-permute-done.2.refs_1_, f32[512,512]{1,0:T(8,128)} %collective-permute-done.9.refs_2_, f32[24,256]{1,0:T(8,128)S(1)} %pad.27.refs_3_.refs_1_), custom_call_target="tpu_custom_call" | custom-call | flops 1 | bytes 1 | tf_op jit(solution)/shard_map/column_step_all/pallas_call | solution.py:152
  190.2 3.0 %correct.6.refs_3_ = f32[2048,512]{1,0:T(8,128)} custom-call(f32[512,512]{1,0:T(8,128)S(1)} %copy-done.5, f32[512,512]{1,0:T(8,128)} %collective-permute-done.16.refs_1_, f32[2048,128]{1,0:T(8,128)S(1)} %bitcast.37, f32[128,512]{1,0:T(8,128)S(1)} %fusion.26.refs_3_.refs_2_, f32[2048,512]{1,0:T(8,128)} %correct.5.refs_4_), custom_call_target="tpu_custom_call", output_to_operand_aliasing={{}: (4, {})} | custom-call | flops 1 | bytes 1 | tf_op jit(solution)/shard_map/correct/pallas_call | solution.py:178
  193.8 1.9 correct.7
  (134 shorter events, 40.6 us)
Async XLA Ops:
  0.6 8.5 %copy-start.25 = (f32[16384]{0:T(1024)S(1)}, f32[16384]{0:T(1024)}, u32[]{:S(2)}) copy-start(f32[16384]{0:T(1024)} %param.10) | copy-start | bytes 196612
  0.6 8.7 %copy-start.22 = (f32[64,256]{1,0:T(8,128)S(1)}, f32[64,256]{1,0:T(8,128)}, u32[]{:S(2)}) copy-start(f32[64,256]{1,0:T(8,128)} %param.13) | copy-start | bytes 196612
  0.7 8.7 %copy-start.24 = (f32[64,256]{1,0:T(8,128)S(1)}, f32[64,256]{1,0:T(8,128)}, u32[]{:S(2)}) copy-start(f32[64,256]{1,0:T(8,128)} %param.12) | copy-start | bytes 196612
  0.7 8.7 %copy-start.23 = (f32[64,256]{1,0:T(8,128)S(1)}, f32[64,256]{1,0:T(8,128)}, u32[]{:S(2)}) copy-start(f32[64,256]{1,0:T(8,128)} %param.11) | copy-start | bytes 196612
  3.8 26.8 %collective-permute-start.1 = (f32[512,512]{1,0:T(8,128)}, f32[512,512]{1,0:T(8,128)}, u32[]{:S(2)}, u32[]{:S(2)}) collective-permute-start(f32[512,512]{1,0:T(8,128)} %get-tuple-element.43), channel_id=1, source_target_pairs={{32,0},{64,32},{96,64},{128,96},{160,128},{192,160},{224,192},{33,... | collective-permute-start | bytes 3145736 | tf_op jit(solution)/shard_map/ppermute | solution.py:339
  5.1 25.6 %collective-permute-start = (f32[512,512]{1,0:T(8,128)}, f32[512,512]{1,0:T(8,128)}, u32[]{:S(2)}, u32[]{:S(2)}) collective-permute-start(f32[512,512]{1,0:T(8,128)} %get-tuple-element.44), channel_id=1, source_target_pairs={{0,32},{32,64},{64,96},{96,128},{128,160},{160,192},{192,224},{1,3... | collective-permute-start | bytes 3145736 | tf_op jit(solution)/shard_map/ppermute | solution.py:338
  9.6 8.7 %copy-start.15 = (f32[5,64,256]{2,1,0:T(8,128)}, f32[5,64,256]{2,1,0:T(8,128)S(1)}, u32[]{:S(2)}) copy-start(f32[5,64,256]{2,1,0:T(8,128)S(1)} %bitcast_dynamic-update-slice_fusion) | copy-start | bytes 983044
  11.2 6.9 %copy-start.26 = (s32[128,16]{0,1:T(8,128)S(1)}, s32[128,16]{0,1:T(8,128)}, u32[]{:S(2)}) copy-start(s32[128,16]{0,1:T(8,128)} %param.14) | copy-start | bytes 24580
  11.2 7.0 %copy-start.27 = (f32[128,16]{0,1:T(8,128)S(1)}, f32[128,16]{0,1:T(8,128)}, u32[]{:S(2)}) copy-start(f32[128,16]{0,1:T(8,128)} %param.15) | copy-start | bytes 24580
  17.9 40.4 %collective-permute-start.4 = (f32[512,512]{1,0:T(8,128)}, f32[512,512]{1,0:T(8,128)}, u32[]{:S(2)}, u32[]{:S(2)}) collective-permute-start(f32[512,512]{1,0:T(8,128)} %get-tuple-element.31.refs_0_), channel_id=1, source_target_pairs={{0,1},{1,0},{2,3},{3,2},{4,5},{5,4},{6,7},{7,6},{8,9},{9,8},{10,11... | collective-permute-start | bytes 3145736 | tf_op jit(solution)/shard_map/ppermute | solution.py:359
  22.7 31.3 %collective-permute-start.3 = (f32[512,512]{1,0:T(8,128)}, f32[512,512]{1,0:T(8,128)}, u32[]{:S(2)}, u32[]{:S(2)}) collective-permute-start(f32[512,512]{1,0:T(8,128)} %get-tuple-element.29.refs_1_.refs_0_), channel_id=1, source_target_pairs={{1,3},{3,5},{5,7},{7,9},{9,11},{11,13},{13,15},{15,17},{17,19},{19... | collective-permute-start | bytes 3145736 | tf_op jit(solution)/shard_map/ppermute | solution.py:360
  43.2 8.4 %copy-start.7 = (f32[512,512]{1,0:T(8,128)S(1)}, f32[512,512]{1,0:T(8,128)}, u32[]{:S(2)}) copy-start(f32[512,512]{1,0:T(8,128)} %get-tuple-element.20.refs_0_) | copy-start | bytes 3145732
  43.2 10.2 %copy-start.16 = (f32[5,64,256]{2,1,0:T(8,128)S(1)}, f32[5,64,256]{2,1,0:T(8,128)}, u32[]{:S(2)}) copy-start(f32[5,64,256]{2,1,0:T(8,128)} %copy-done.15) | copy-start | bytes 983044
  43.2 10.9 %copy-start.1 = (f32[512,512]{1,0:T(8,128)S(1)}, f32[512,512]{1,0:T(8,128)}, u32[]{:S(2)}) copy-start(f32[512,512]{1,0:T(8,128)} %get-tuple-element.29.refs_1_.refs_0_) | copy-start | bytes 3145732
  44.3 21.5 %all-to-all-start = ((f32[16,128,128]{2,1,0:T(8,128)}), f32[16,128,128]{2,1,0:T(8,128)}, u32[]{:S(2)}, u32[]{:S(2)}) async-start(f32[16,128,128]{2,1,0:T(8,128)} %bitcast.9), calls=%async_computation | async-start | bytes 2097152 | tf_op jit(solution)/shard_map/all_to_all | solution.py:394
  51.6 29.6 %collective-permute-start.2 = (f32[512,512]{1,0:T(8,128)S(1)}, f32[512,512]{1,0:T(8,128)}, u32[]{:S(2)}, u32[]{:S(2)}) collective-permute-start(f32[512,512]{1,0:T(8,128)S(1)} %copy-done.7), channel_id=1, source_target_pairs={{0,1},{1,0},{2,3},{3,2},{4,5},{5,4},{6,7},{7,6},{8,9},{9,8},{10,11... | collective-permute-start | bytes 3145736 | tf_op jit(solution)/shard_map/ppermute | solution.py:372
  54.0 18.2 %copy-start.3 = (f32[512,512]{1,0:T(8,128)S(1)}, f32[512,512]{1,0:T(8,128)}, u32[]{:S(2)}) copy-start(f32[512,512]{1,0:T(8,128)} %get-tuple-element.30.refs_1_.refs_0_) | copy-start | bytes 3145732
  67.7 12.6 %collective-permute-start.5 = (f32[128,128]{1,0:T(8,128)}, f32[128,128]{1,0:T(8,128)}, u32[]{:S(2)}, u32[]{:S(2)}) collective-permute-start(f32[128,128]{1,0:T(8,128)} %reduce_sum.47), channel_id=1, source_target_pairs={{0,1},{1,0},{2,3},{3,2},{4,5},{5,4},{6,7},{7,6},{8,9},{9,8},{10,11... | collective-permute-start | bytes 196616 | tf_op jit(solution)/shard_map/ppermute | solution.py:401
  72.2 37.2 %collective-permute-start.6 = (f32[512,512]{1,0:T(8,128)S(1)}, f32[512,512]{1,0:T(8,128)}, u32[]{:S(2)}, u32[]{:S(2)}) collective-permute-start(f32[512,512]{1,0:T(8,128)S(1)} %copy-done.3), channel_id=1, source_target_pairs={{1,3},{3,5},{5,7},{7,9},{9,11},{11,13},{13,15},{15,17},{17,19},{19... | collective-permute-start | bytes 3145736 | tf_op jit(solution)/shard_map/ppermute | solution.py:373
  74.7 38.9 %collective-permute-start.8 = (f32[512,512]{1,0:T(8,128)}, f32[512,512]{1,0:T(8,128)}, u32[]{:S(2)}, u32[]{:S(2)}) collective-permute-start(f32[512,512]{1,0:T(8,128)} %collective-permute-done.4.refs_1_), channel_id=1, source_target_pairs={{0,2},{2,4},{4,6},{6,8},{8,10},{10,12},{12,14},{14,16},{16,18},{18... | collective-permute-start | bytes 3145736 | tf_op jit(solution)/shard_map/ppermute | solution.py:397
  80.2 33.5 %collective-permute-start.7 = (f32[512,512]{1,0:T(8,128)}, f32[512,512]{1,0:T(8,128)}, u32[]{:S(2)}, u32[]{:S(2)}) collective-permute-start(f32[512,512]{1,0:T(8,128)} %copy-done.14), channel_id=1, source_target_pairs={{0,1},{1,0},{2,3},{3,2},{4,5},{5,4},{6,7},{7,6},{8,9},{9,8},{10,11... | collective-permute-start | bytes 3145736 | tf_op jit(solution)/shard_map/ppermute | solution.py:402
  82.3 38.6 %all-to-all-start.1 = ((f32[16,128,128]{2,1,0:T(8,128)}), f32[16,128,128]{2,1,0:T(8,128)S(1)}, u32[]{:S(2)}, u32[]{:S(2)}) async-start(f32[16,128,128]{2,1,0:T(8,128)} %broadcast_in_dim.33), calls=%async_computation.1 | async-start | bytes 2097152 | tf_op jit(solution)/shard_map/all_to_all | solution.py:404
  88.1 9.9 %copy-start.28 = (f32[128]{0:T(128)S(1)}, f32[128]{0:T(128)}, u32[]{:S(2)}) copy-start(f32[128]{0:T(128)} %param.16) | copy-start | bytes 1540
  124.0 6.5 %collective-permute-start.10 = (f32[640,128]{1,0:T(8,128)S(1)}, f32[640,128]{1,0:T(8,128)}, u32[]{:S(2)}, u32[]{:S(2)}) collective-permute-start(f32[640,128]{1,0:T(8,128)S(1)} %pad_maximum_fusion.1), channel_id=1, source_target_pairs={{0,32},{32,0},{64,96},{96,64},{128,160},{160,128},{192,224},{224,1... | collective-permute-start | bytes 983048 | tf_op jit(solution)/shard_map/ppermute | solution.py:419
  124.1 32.8 %collective-permute-start.9 = (f32[512,512]{1,0:T(8,128)}, f32[512,512]{1,0:T(8,128)}, u32[]{:S(2)}, u32[]{:S(2)}) collective-permute-start(f32[512,512]{1,0:T(8,128)} %collective-permute-done.2.refs_1_), channel_id=1, source_target_pairs={{0,2},{2,4},{4,6},{6,8},{8,10},{10,12},{12,14},{14,16},{16,18},{18... | collective-permute-start | bytes 3145736 | tf_op jit(solution)/shard_map/ppermute | solution.py:413
  131.6 8.1 %collective-permute-start.11 = (f32[128,128]{1,0:T(8,128)S(1)}, f32[128,128]{1,0:T(8,128)S(1)}, u32[]{:S(2)}, u32[]{:S(2)}) collective-permute-start(f32[128,128]{1,0:T(8,128)S(1)} %slice.98), channel_id=1, source_target_pairs={{0,64},{32,96},{64,0},{96,32},{128,192},{160,224},{192,128},{224,1... | collective-permute-start | bytes 196616 | tf_op jit(solution)/shard_map/ppermute | solution.py:421
  135.7 19.2 %collective-permute-start.14 = (f32[512,128]{1,0:T(8,128)}, f32[512,128]{1,0:T(8,128)}, u32[]{:S(2)}, u32[]{:S(2)}) collective-permute-start(f32[512,128]{1,0:T(8,128)} %slice_select_fusion), channel_id=1, source_target_pairs={{0,128},{32,160},{1,129},{33,161},{2,130},{34,162},{3,131},{35,163... | collective-permute-start | bytes 786440 | tf_op jit(solution)/shard_map/ppermute | solution.py:432
  137.1 18.7 %collective-permute-start.15 = (f32[512,128]{1,0:T(8,128)}, f32[512,128]{1,0:T(8,128)}, u32[]{:S(2)}, u32[]{:S(2)}) collective-permute-start(f32[512,128]{1,0:T(8,128)} %slice_select_fusion), channel_id=1, source_target_pairs={{0,192},{32,224},{1,193},{33,225},{2,194},{34,226},{3,195},{35,227... | collective-permute-start | bytes 786440 | tf_op jit(solution)/shard_map/ppermute | solution.py:432
  138.4 17.4 %collective-permute-start.13 = (f32[512,128]{1,0:T(8,128)}, f32[512,128]{1,0:T(8,128)}, u32[]{:S(2)}, u32[]{:S(2)}) collective-permute-start(f32[512,128]{1,0:T(8,128)} %slice_select_fusion), channel_id=1, source_target_pairs={{0,64},{32,96},{1,65},{33,97},{2,66},{34,98},{3,67},{35,99},{4,68}... | collective-permute-start | bytes 786440 | tf_op jit(solution)/shard_map/ppermute | solution.py:432
  140.4 12.9 %collective-permute-start.12 = (f32[128,128]{1,0:T(8,128)}, f32[128,128]{1,0:T(8,128)}, u32[]{:S(2)}, u32[]{:S(2)}) collective-permute-start(f32[128,128]{1,0:T(8,128)} %slice_add_fusion), channel_id=1, source_target_pairs={{0,128},{32,160},{64,192},{96,224},{128,0},{160,32},{192,64},{224,... | collective-permute-start | bytes 196616 | tf_op jit(solution)/shard_map/ppermute | solution.py:422
  142.5 6.6 %copy-start.10 = (f32[512,512]{1,0:T(8,128)S(1)}, f32[512,512]{1,0:T(8,128)}, u32[]{:S(2)}) copy-start(f32[512,512]{1,0:T(8,128)} %get-tuple-element.31.refs_0_) | copy-start | bytes 3145732
  156.9 33.3 %collective-permute-start.16 = (f32[512,512]{1,0:T(8,128)}, f32[512,512]{1,0:T(8,128)}, u32[]{:S(2)}, u32[]{:S(2)}) collective-permute-start(f32[512,512]{1,0:T(8,128)} %column_step_others.3), channel_id=1, source_target_pairs={{0,1},{1,0},{2,3},{3,2},{4,5},{5,4},{6,7},{7,6},{8,9},{9,8},{10,11... | collective-permute-start | bytes 3145736 | tf_op jit(solution)/shard_map/ppermute | solution.py:439
  (16 other events, 26.0 us)
where the time goes:
time: 197 us; the launch traced here: 196 us
  Pallas kernels  71.3 us (36%)
  starting transfers between devices  59.6 us (30%)
  waiting for transfers between devices  27 us (14%)
  local copies, waits for them, and re-layouts  20.1 us (10%)
  other arithmetic  11.3 us (6%)
  matrix products  5.22 us (3%)
    pallas_call x6, Pallas kernels, column_step(): pl.pallas_call(functools.partial(column_kernel, mode, block), grid=(rows...  20.8 us
    pallas_call x2, Pallas kernels, row_steps(): pl.pallas_call(functools.partial(row_kernel, groups, len(arrays), outs),...  14.9 us
    pallas_call x1, Pallas kernels, inverse(): pl.pallas_call(inverse_kernel, in_specs=[vmem, vmem], out_specs=vmem, out...  12.4 us
    unnamed x65, local copies, waits for them, and re-layouts  12.3 us
    ppermute x1, waiting for transfers between devices, shards(): raw_b2 = lax.ppermute(b2, 'cols', back)  11.5 us
    pallas_call x4, Pallas kernels, correct(): pl.pallas_call(functools.partial(correct_kernel, n), grid=(rows // LON,),...  9.89 us
    ppermute x1, starting transfers between devices, shards(): sum_b2 = lax.ppermute(after(part_b2, gram), 'cols', swap)  7.9 us
    all_to_all x1, waiting for transfers between devices, shards(): lax.all_to_all(v_part.reshape(16, 128, OBS), 'cols', 0, 0, axis_index_gro...  7.36 us
  transfers between devices with their start and end apart: 19, of which 4 were waited for; matrix products, arithmetic and copies ran while one was open for 10% of the time, Pallas kernels for 34%

commit v1 on v0

--- a/solution.py
+++ b/solution.py
@@ -82,7 +82,7 @@
             pltpu.VMEM((5, total, LON, 128), jnp.float32),
             pltpu.VMEM((max(n for _, _, n in groups) + 2, LON, 128), jnp.float32),
         ],
-        compiler_params=pltpu.CompilerParams(vmem_limit_bytes=60 << 20),
+        compiler_params=pltpu.CompilerParams(vmem_limit_bytes=16 << 20),
         cost_estimate=SMALL,
         name="row_step",
     )(*arrays, coef)
@@ -158,7 +158,7 @@
         out_specs=spec,
         out_shape=jax.ShapeDtypeStruct((rows, 2 * LON), jnp.float32),
         scratch_shapes=[pltpu.VMEM((20, 8, LON), jnp.float32)],
-        compiler_params=pltpu.CompilerParams(vmem_limit_bytes=40 << 20),
+        compiler_params=pltpu.CompilerParams(vmem_limit_bytes=16 << 20),
         cost_estimate=SMALL,
         name="column_step_" + mode,
     )(flag, *blocks, coef)
@@ -187,7 +187,7 @@
         out_specs=pl.BlockSpec((LON, 2 * LON), lambda i: (first_lat + i, 0)),
         out_shape=jax.ShapeDtypeStruct((8 * LON, 2 * LON), jnp.float32),
         input_output_aliases={n + 2: 0} if aliased else {},
-        compiler_params=pltpu.CompilerParams(vmem_limit_bytes=40 << 20),
+        compiler_params=pltpu.CompilerParams(vmem_limit_bytes=16 << 20),
         cost_estimate=SMALL,
         name="correct",
     )(*terms, left, right, *aliased)
@@ -230,7 +230,7 @@
         out_specs=vmem,
         out_shape=jax.ShapeDtypeStruct((OBS, n * LON), jnp.float32),
         scratch_shapes=[pltpu.VMEM((n + 4, OBS, LON), jnp.float32)] * 2,
-        compiler_params=pltpu.CompilerParams(vmem_limit_bytes=40 << 20),
+        compiler_params=pltpu.CompilerParams(vmem_limit_bytes=16 << 20),
         cost_estimate=SMALL,
         name="adjoint_footprints",
     )(start, position, share, coef)
@@ -254,7 +254,7 @@
         in_specs=[pl.BlockSpec(memory_space=pltpu.SMEM), vmem, vmem],
         out_specs=vmem,
         out_shape=jax.ShapeDtypeStruct((OBS, lats * LON), jnp.float32),
-        compiler_params=pltpu.CompilerParams(vmem_limit_bytes=40 << 20),
+        compiler_params=pltpu.CompilerParams(vmem_limit_bytes=16 << 20),
         cost_estimate=SMALL,
         name="footprints",
     )(start, position, share)
@@ -283,7 +283,7 @@
         in_specs=[vmem] * (len(blocks) + 1),
         out_specs=vmem,
         out_shape=jax.ShapeDtypeStruct((rows, OBS), jnp.float32),
-        compiler_params=pltpu.CompilerParams(vmem_limit_bytes=40 << 20),
+        compiler_params=pltpu.CompilerParams(vmem_limit_bytes=16 << 20),
         cost_estimate=SMALL,
         name="project",
     )(*blocks, g)

time: 197 us -> 193 us (0.980)
  Pallas kernels: 71.3 us -> 68.5 us
    pallas_call x2, Pallas kernels: 14.9 us -> 10.8 us  [row_steps(): pl.pallas_call(functools.partial(row_kernel, groups, len(arrays), outs),...]
    ppermute x1, starting transfers between devices: 3.33 us -> 0.09 us  [shards(): lax.ppermute(gram, 'rows', [(i, i ^ 2) for i in range(rows_n)])]
    unnamed x65 -> x75, local copies, waits for them, and re-layouts: 12.3 us -> 12.9 us
  transfers between devices with their start and end apart: 19 -> 19, of which waited for: 4 -> 6; matrix products, arithmetic and copies ran while one was open for 10% -> 10% of each run, Pallas kernels for 34% -> 33%
where the time goes in v1:
time: 193 us; the launch traced here: 191 us
  Pallas kernels  68.5 us (35%)
  starting transfers between devices  57.8 us (30%)
  waiting for transfers between devices  26.3 us (14%)
  local copies, waits for them, and re-layouts  20.7 us (11%)
  other arithmetic  11.1 us (6%)
  matrix products  5.22 us (3%)
    pallas_call x6, Pallas kernels, column_step(): pl.pallas_call(functools.partial(column_kernel, mode, block), grid=(rows...  20.9 us
    unnamed x75, local copies, waits for them, and re-layouts  12.9 us
    pallas_call x1, Pallas kernels, inverse(): pl.pallas_call(inverse_kernel, in_specs=[vmem, vmem], out_specs=vmem, out...  12.4 us
    ppermute x1, waiting for transfers between devices, shards(): raw_b2 = lax.ppermute(b2, 'cols', back)  11.4 us
    pallas_call x2, Pallas kernels, row_steps(): pl.pallas_call(functools.partial(row_kernel, groups, len(arrays), outs),...  10.8 us
    pallas_call x4, Pallas kernels, correct(): pl.pallas_call(functools.partial(correct_kernel, n), grid=(rows // LON,),...  9.99 us
    ppermute x1, starting transfers between devices, shards(): sum_b2 = lax.ppermute(after(part_b2, gram), 'cols', swap)  8.03 us
    all_to_all x1, starting transfers between devices, shards(): lax.all_to_all(v_part.reshape(16, 128, OBS), 'cols', 0, 0, axis_index_gro...  7.32 us
  transfers between devices with their start and end apart: 19, of which 6 were waited for; matrix products, arithmetic and copies ran while one was open for 10% of the time, Pallas kernels for 33%

profile of v1, /device:TPU:34, one launch (start us, length us, event | category | flops | bytes accessed | tf_op | source)
XLA Modules:
  0.0 191.1 jit_solution(4058588037093341296)
XLA Ops:
  0.7 3.1 %fusion.19 = (f32[512,512]{1,0:T(8,128)}, f32[512,512]{1,0:T(8,128)}) fusion(f32[2048,512]{1,0:T(8,128)} %refs_0_.1), kind=kLoop, calls=%fused_computation.61 | loop fusion | bytes 4194304 | tf_op jit(solution)/shard_map/slice | solution.py:339
  5.1 4.0 %collective-permute-start = (f32[512,512]{1,0:T(8,128)}, f32[512,512]{1,0:T(8,128)}, u32[]{:S(2)}, u32[]{:S(2)}) collective-permute-start(f32[512,512]{1,0:T(8,128)} %get-tuple-element.44), channel_id=1, source_target_pairs={{0,32},{32,64},{64,96},{96,128},{128,160},{160,192},{192,224},{1,3... | collective-permute-start | bytes 3145736 | tf_op jit(solution)/shard_map/ppermute | solution.py:338
  12.0 2.2 %copy-done = f32[2048,512]{1,0:T(8,128)S(1)} copy-done((f32[2048,512]{1,0:T(8,128)S(1)}, f32[2048,512]{1,0:T(8,128)}, u32[]{:S(2)}) %copy-start) | copy-done | bytes 4194328
  14.2 4.6 %row_step.3 = (f32[512,512]{1,0:T(8,128)}, f32[512,512]{1,0:T(8,128)S(1)}) custom-call(f32[2048,512]{1,0:T(8,128)S(1)} %copy-done, f32[2560,8]{1,0:T(8,128)S(1)} %pad.23.refs_3_.refs_1_), custom_call_target="tpu_custom_call" | custom-call | flops 1 | bytes 1 | tf_op jit(solution)/shard_map/row_step/pallas_call | solution.py:74
  20.1 4.4 %adjoint_footprints.1.refs_2_ = f32[128,512]{1,0:T(8,128)S(1)} custom-call(s32[1]{0:T(128)} %bitcast.8.start, s32[128,16]{1,0:T(8,128)S(1)} %copy.22.position, f32[128,16]{1,0:T(8,128)S(1)} %copy.23.share, f32[30,256]{1,0:T(8,128)S(1)} %reshape.128.coef), custom_call_target="tpu_custom_call" | custom-call | flops 1 | bytes 1 | tf_op jit(solution)/shard_map/adjoint_footprints/pallas_call | solution.py:227
  24.5 3.7 %collective-permute-start.3 = (f32[512,512]{1,0:T(8,128)S(1)}, f32[512,512]{1,0:T(8,128)}, u32[]{:S(2)}, u32[]{:S(2)}) collective-permute-start(f32[512,512]{1,0:T(8,128)S(1)} %get-tuple-element.29.refs_1_.refs_0_), channel_id=1, source_target_pairs={{1,3},{3,5},{5,7},{7,9},{9,11},{11,13},{13,15},{15,17},{17,19},{19... | collective-permute-start | bytes 3145736 | tf_op jit(solution)/shard_map/ppermute | solution.py:360
  28.2 3.0 %project.3 = f32[1024,128]{1,0:T(8,128)S(1)} custom-call(f32[512,512]{1,0:T(8,128)} %get-tuple-element.31.refs_0_, f32[512,512]{1,0:T(8,128)S(1)} %get-tuple-element.29.refs_1_.refs_0_, f32[128,512]{1,0:T(8,128)S(1)} %adjoint_footprints.1.refs_2_), custom_call_target="tpu_custom_call" | custom-call | flops 1 | bytes 1 | tf_op jit(solution)/shard_map/project/pallas_call | solution.py:281
  31.2 2.2 %copy-done.1 = f32[2048,512]{1,0:T(8,128)S(1)} copy-done((f32[2048,512]{1,0:T(8,128)S(1)}, f32[2048,512]{1,0:T(8,128)}, u32[]{:S(2)}) %copy-start.1) | copy-done | bytes 4194328
  33.4 6.2 %row_step.2 = (f32[512,512]{1,0:T(8,128)S(1)}, f32[512,512]{1,0:T(8,128)S(1)}) custom-call(f32[512,512]{1,0:T(8,128)} %collective-permute-done.refs_0_, f32[2048,512]{1,0:T(8,128)S(1)} %copy-done.1, f32[512,512]{1,0:T(8,128)} %collective-permute-done.1.refs_2_, f32[2560,8]{1,0:T(8,128)S(1)} %pad.23.refs_3_.refs_1_), custom_call_target="tpu_custom_call" | custom-call | flops 1 | bytes 1 | tf_op jit(solution)/shard_map/row_step/pallas_call | solution.py:74
  42.5 7.3 %all-to-all-start = ((f32[16,128,128]{2,1,0:T(8,128)}), f32[16,128,128]{2,1,0:T(8,128)}, u32[]{:S(2)}, u32[]{:S(2)}) async-start(f32[16,128,128]{2,1,0:T(8,128)} %bitcast.40), calls=%async_computation | async-start | bytes 2097152 | tf_op jit(solution)/shard_map/all_to_all | solution.py:394
  53.8 3.2 %column_step_others.2 = f32[512,512]{1,0:T(8,128)S(1)} custom-call(s32[1]{0:T(128)S(6)} %sub.35.flag, f32[512,512]{1,0:T(8,128)S(1)} %get-tuple-element.29.refs_1_.refs_0_, f32[512,512]{1,0:T(8,128)} %collective-permute-done.3.refs_1_, f32[24,256]{1,0:T(8,128)S(1)} %pad.24.refs_2_), custom_call_target="tpu_custom_call" | custom-call | flops 1 | bytes 1 | tf_op jit(solution)/shard_map/column_step_others/pallas_call | solution.py:152
  58.1 6.4 %all-to-all-done = f32[16,128,128]{2,1,0:T(8,128)} async-done(((f32[16,128,128]{2,1,0:T(8,128)}), f32[16,128,128]{2,1,0:T(8,128)}, u32[]{:S(2)}, u32[]{:S(2)}) %all-to-all-start) | async-done | bytes 1048608 | tf_op jit(solution)/shard_map/all_to_all | solution.py:394
  65.8 4.1 %collective-permute-start.5 = (f32[128,128]{1,0:T(8,128)S(1)}, f32[128,128]{1,0:T(8,128)S(1)}, u32[]{:S(2)}, u32[]{:S(2)}) collective-permute-start(f32[128,128]{1,0:T(8,128)S(1)} %reduce_sum.47), channel_id=1, source_target_pairs={{0,1},{1,0},{2,3},{3,2},{4,5},{5,4},{6,7},{7,6},{8,9},{9,8},{10,11... | collective-permute-start | bytes 196616 | tf_op jit(solution)/shard_map/ppermute | solution.py:401
  70.0 2.5 %collective-permute-start.6 = (f32[512,512]{1,0:T(8,128)S(1)}, f32[512,512]{1,0:T(8,128)}, u32[]{:S(2)}, u32[]{:S(2)}) collective-permute-start(f32[512,512]{1,0:T(8,128)S(1)} %get-tuple-element.30.refs_1_.refs_0_), channel_id=1, source_target_pairs={{1,3},{3,5},{5,7},{7,9},{9,11},{11,13},{13,15},{15,17},{17,19},{19... | collective-permute-start | bytes 3145736 | tf_op jit(solution)/shard_map/ppermute | solution.py:373
  72.4 5.5 %collective-permute-start.8 = (f32[512,512]{1,0:T(8,128)}, f32[512,512]{1,0:T(8,128)}, u32[]{:S(2)}, u32[]{:S(2)}) collective-permute-start(f32[512,512]{1,0:T(8,128)} %collective-permute-done.4.refs_1_), channel_id=1, source_target_pairs={{0,2},{2,4},{4,6},{6,8},{8,10},{10,12},{12,14},{14,16},{16,18},{18... | collective-permute-start | bytes 3145736 | tf_op jit(solution)/shard_map/ppermute | solution.py:397
  79.2 6.2 %all-to-all-start.1 = ((f32[16,128,128]{2,1,0:T(8,128)}), f32[16,128,128]{2,1,0:T(8,128)S(1)}, u32[]{:S(2)}, u32[]{:S(2)}) async-start(f32[16,128,128]{2,1,0:T(8,128)} %broadcast_in_dim.33), calls=%async_computation.1 | async-start | bytes 2097152 | tf_op jit(solution)/shard_map/all_to_all | solution.py:404
  85.4 5.2 %footprints.1 = f32[128,2048]{1,0:T(8,128)S(1)} custom-call(s32[1]{0:T(128)} %bitcast.11.start, s32[128,16]{1,0:T(8,128)S(1)} %copy.22.position, f32[128,16]{1,0:T(8,128)S(1)} %copy.23.share), custom_call_target="tpu_custom_call" | custom-call | flops 1 | bytes 1 | tf_op jit(solution)/shard_map/footprints/pallas_call | solution.py:252
  95.9 11.4 %collective-permute-done.6.refs_1_ = f32[512,512]{1,0:T(8,128)} collective-permute-done((f32[512,512]{1,0:T(8,128)S(1)}, f32[512,512]{1,0:T(8,128)}, u32[]{:S(2)}, u32[]{:S(2)}) %collective-permute-start.6) | collective-permute-done | bytes 1048608 | tf_op jit(solution)/shard_map/ppermute | solution.py:373
  107.2 4.2 %column_step_others.3 = f32[512,512]{1,0:T(8,128)} custom-call(s32[1]{0:T(128)S(6)} %sub.35.flag, f32[512,512]{1,0:T(8,128)S(1)} %get-tuple-element.30.refs_1_.refs_0_, f32[512,512]{1,0:T(8,128)} %collective-permute-done.6.refs_1_, f32[24,256]{1,0:T(8,128)S(1)} %pad.24.refs_2_), custom_call_target="tpu_custom_call" | custom-call | flops 1 | bytes 1 | tf_op jit(solution)/shard_map/column_step_others/pallas_call | solution.py:152
  111.4 7.2 %all-to-all-done.1 = f32[16,128,128]{2,1,0:T(8,128)S(1)} async-done(((f32[16,128,128]{2,1,0:T(8,128)}), f32[16,128,128]{2,1,0:T(8,128)S(1)}, u32[]{:S(2)}, u32[]{:S(2)}) %all-to-all-start.1) | async-done | bytes 1048608 | tf_op jit(solution)/shard_map/all_to_all | solution.py:404
  118.6 2.4 %fusion.25 = f32[128,128]{1,0:T(8,128)S(1)} fusion(f32[128,2048]{1,0:T(8,128)} %copy-done.7, f32[2048,128]{1,0:T(8,128)S(1)} %bitcast.33), kind=kOutput, calls=%fused_computation.67 | convolution fusion | flops 402653184 | bytes 2162688 | tf_op jit(solution)/shard_map/dot_general | solution.py:415
  121.9 6.4 %collective-permute-start.9 = (f32[512,512]{1,0:T(8,128)}, f32[512,512]{1,0:T(8,128)}, u32[]{:S(2)}, u32[]{:S(2)}) collective-permute-start(f32[512,512]{1,0:T(8,128)} %collective-permute-done.2.refs_1_), channel_id=1, source_target_pairs={{0,2},{2,4},{4,6},{6,8},{8,10},{10,12},{12,14},{14,16},{16,18},{18... | collective-permute-start | bytes 3145736 | tf_op jit(solution)/shard_map/ppermute | solution.py:413
  135.3 2.7 %collective-permute-start.12 = (f32[128,128]{1,0:T(8,128)}, f32[128,128]{1,0:T(8,128)}, u32[]{:S(2)}, u32[]{:S(2)}) collective-permute-start(f32[128,128]{1,0:T(8,128)} %slice_add_fusion), channel_id=1, source_target_pairs={{0,128},{32,160},{64,192},{96,224},{128,0},{160,32},{192,64},{224,... | collective-permute-start | bytes 196616 | tf_op jit(solution)/shard_map/ppermute | solution.py:422
  138.1 2.3 %column_step_own.3.refs_0_ = f32[512,512]{1,0:T(8,128)S(1)} custom-call(s32[1]{0:T(128)} %bitcast.flag, f32[512,512]{1,0:T(8,128)S(1)} %get-tuple-element.30.refs_1_.refs_0_, f32[24,256]{1,0:T(8,128)S(1)} %pad.27.refs_3_.refs_1_), custom_call_target="tpu_custom_call" | custom-call | flops 1 | bytes 1 | tf_op jit(solution)/shard_map/column_step_own/pallas_call | solution.py:152
  141.3 2.3 %column_step_own.2.refs_0_ = f32[512,512]{1,0:T(8,128)S(1)} custom-call(s32[1]{0:T(128)} %bitcast.flag, f32[512,512]{1,0:T(8,128)S(1)} %get-tuple-element.29.refs_1_.refs_0_, f32[24,256]{1,0:T(8,128)S(1)} %pad.27.refs_3_.refs_1_), custom_call_target="tpu_custom_call" | custom-call | flops 1 | bytes 1 | tf_op jit(solution)/shard_map/column_step_own/pallas_call | solution.py:152
  144.6 4.5 %column_step_all.3.refs_0_ = f32[512,512]{1,0:T(8,128)S(1)} custom-call(s32[1]{0:T(128)} %bitcast.flag, f32[512,512]{1,0:T(8,128)} %get-tuple-element.31.refs_0_, f32[512,512]{1,0:T(8,128)} %collective-permute-done.4.refs_1_, f32[512,512]{1,0:T(8,128)} %collective-permute-done.8.refs_2_, f32[24,256]{1,0:T(8,128)S(1)} %pad.27.refs_3_.refs_1_), custom_call_target="tpu_custom_call" | custom-call | flops 1 | bytes 1 | tf_op jit(solution)/shard_map/column_step_all/pallas_call | solution.py:152
  153.2 8.0 %collective-permute-start.16 = (f32[512,512]{1,0:T(8,128)}, f32[512,512]{1,0:T(8,128)}, u32[]{:S(2)}, u32[]{:S(2)}) collective-permute-start(f32[512,512]{1,0:T(8,128)} %column_step_others.3), channel_id=1, source_target_pairs={{0,1},{1,0},{2,3},{3,2},{4,5},{5,4},{6,7},{7,6},{8,9},{9,8},{10,11... | collective-permute-start | bytes 3145736 | tf_op jit(solution)/shard_map/ppermute | solution.py:439
  162.0 12.4 %inverse.1 = f32[128,128]{1,0:T(8,128)} custom-call(f32[128,128]{1,0:T(8,128)} %add.149.gram, f32[1,128]{1,0:T(1,128)} %bitcast.42), custom_call_target="tpu_custom_call" | custom-call | flops 1 | bytes 1 | tf_op jit(solution)/shard_map/inverse/pallas_call | solution.py:308
  175.6 3.1 %correct.4.refs_3_ = f32[2048,512]{1,0:T(8,128)} custom-call(f32[512,512]{1,0:T(8,128)S(1)} %copy-done.11, f32[512,512]{1,0:T(8,128)} %collective-permute-done.7.refs_1_, f32[2048,128]{1,0:T(8,128)S(1)} %bitcast.35, f32[128,512]{1,0:T(8,128)S(1)} %fusion.26.refs_3_.refs_2_), custom_call_target="tpu_custom_call" | custom-call | flops 1 | bytes 1 | tf_op jit(solution)/shard_map/correct/pallas_call | solution.py:178
  180.6 4.4 %column_step_all.2.refs_0_ = f32[512,512]{1,0:T(8,128)S(1)} custom-call(s32[1]{0:T(128)} %bitcast.flag, f32[512,512]{1,0:T(8,128)S(1)} %copy-done.6, f32[512,512]{1,0:T(8,128)} %collective-permute-done.2.refs_1_, f32[512,512]{1,0:T(8,128)} %collective-permute-done.9.refs_2_, f32[24,256]{1,0:T(8,128)S(1)} %pad.27.refs_3_.refs_1_), custom_call_target="tpu_custom_call" | custom-call | flops 1 | bytes 1 | tf_op jit(solution)/shard_map/column_step_all/pallas_call | solution.py:152
  185.5 3.0 %correct.6.refs_3_ = f32[2048,512]{1,0:T(8,128)} custom-call(f32[512,512]{1,0:T(8,128)S(1)} %copy-done.3, f32[512,512]{1,0:T(8,128)} %collective-permute-done.16.refs_1_, f32[2048,128]{1,0:T(8,128)S(1)} %bitcast.37, f32[128,512]{1,0:T(8,128)S(1)} %fusion.26.refs_3_.refs_2_, f32[2048,512]{1,0:T(8,128)} %correct.5.refs_4_), custom_call_target="tpu_custom_call", output_to_operand_aliasing={{}: (4, {})} | custom-call | flops 1 | bytes 1 | tf_op jit(solution)/shard_map/correct/pallas_call | solution.py:178
  189.1 1.9 %correct.7 = f32[2048,512]{1,0:T(8,128)} custom-call(f32[512,512]{1,0:T(8,128)S(1)} %column_step_all.2.refs_0_, f32[2048,128]{1,0:T(8,128)S(1)} %bitcast.38, f32[128,512]{1,0:T(8,128)S(1)} %fusion.26.refs_3_.refs_2_, f32[2048,512]{1,0:T(8,128)} %correct.6.refs_3_), custom_call_target="tpu_custom_call", output_to_operand_aliasing={{}: (3, {})} | custom-call | flops 1 | bytes 1 | tf_op jit(solution)/shard_map/correct/pallas_call | solution.py:178
  (144 shorter events, 39.8 us)
Async XLA Ops:
  0.6 8.5 %copy-start.29 = (f32[16384]{0:T(1024)S(1)}, f32[16384]{0:T(1024)}, u32[]{:S(2)}) copy-start(f32[16384]{0:T(1024)} %param.10) | copy-start | bytes 196612
  0.6 8.7 %copy-start.26 = (f32[64,256]{1,0:T(8,128)S(1)}, f32[64,256]{1,0:T(8,128)}, u32[]{:S(2)}) copy-start(f32[64,256]{1,0:T(8,128)} %param.13) | copy-start | bytes 196612
  0.7 8.7 %copy-start.28 = (f32[64,256]{1,0:T(8,128)S(1)}, f32[64,256]{1,0:T(8,128)}, u32[]{:S(2)}) copy-start(f32[64,256]{1,0:T(8,128)} %param.12) | copy-start | bytes 196612
  0.7 8.7 %copy-start.27 = (f32[64,256]{1,0:T(8,128)S(1)}, f32[64,256]{1,0:T(8,128)}, u32[]{:S(2)}) copy-start(f32[64,256]{1,0:T(8,128)} %param.11) | copy-start | bytes 196612
  3.8 27.4 %collective-permute-start.1 = (f32[512,512]{1,0:T(8,128)}, f32[512,512]{1,0:T(8,128)}, u32[]{:S(2)}, u32[]{:S(2)}) collective-permute-start(f32[512,512]{1,0:T(8,128)} %get-tuple-element.43), channel_id=1, source_target_pairs={{32,0},{64,32},{96,64},{128,96},{160,128},{192,160},{224,192},{33,... | collective-permute-start | bytes 3145736 | tf_op jit(solution)/shard_map/ppermute | solution.py:339
  5.1 26.1 %collective-permute-start = (f32[512,512]{1,0:T(8,128)}, f32[512,512]{1,0:T(8,128)}, u32[]{:S(2)}, u32[]{:S(2)}) collective-permute-start(f32[512,512]{1,0:T(8,128)} %get-tuple-element.44), channel_id=1, source_target_pairs={{0,32},{32,64},{64,96},{96,128},{128,160},{160,192},{192,224},{1,3... | collective-permute-start | bytes 3145736 | tf_op jit(solution)/shard_map/ppermute | solution.py:338
  14.2 4.8 %copy-start.31 = (f32[128,16]{0,1:T(8,128)S(1)}, f32[128,16]{0,1:T(8,128)}, u32[]{:S(2)}) copy-start(f32[128,16]{0,1:T(8,128)} %param.15) | copy-start | bytes 24580
  18.8 39.3 %collective-permute-start.4 = (f32[512,512]{1,0:T(8,128)}, f32[512,512]{1,0:T(8,128)}, u32[]{:S(2)}, u32[]{:S(2)}) collective-permute-start(f32[512,512]{1,0:T(8,128)} %get-tuple-element.31.refs_0_), channel_id=1, source_target_pairs={{0,1},{1,0},{2,3},{3,2},{4,5},{5,4},{6,7},{7,6},{8,9},{9,8},{10,11... | collective-permute-start | bytes 3145736 | tf_op jit(solution)/shard_map/ppermute | solution.py:359
  24.5 29.3 %collective-permute-start.3 = (f32[512,512]{1,0:T(8,128)S(1)}, f32[512,512]{1,0:T(8,128)}, u32[]{:S(2)}, u32[]{:S(2)}) collective-permute-start(f32[512,512]{1,0:T(8,128)S(1)} %get-tuple-element.29.refs_1_.refs_0_), channel_id=1, source_target_pairs={{1,3},{3,5},{5,7},{7,9},{9,11},{11,13},{13,15},{15,17},{17,19},{19... | collective-permute-start | bytes 3145736 | tf_op jit(solution)/shard_map/ppermute | solution.py:360
  42.5 7.3 %copy-start.5 = (f32[512,512]{1,0:T(8,128)S(1)}, f32[512,512]{1,0:T(8,128)}, u32[]{:S(2)}) copy-start(f32[512,512]{1,0:T(8,128)} %copy-done.4) | copy-start | bytes 3145732
  42.5 22.0 %all-to-all-start = ((f32[16,128,128]{2,1,0:T(8,128)}), f32[16,128,128]{2,1,0:T(8,128)}, u32[]{:S(2)}, u32[]{:S(2)}) async-start(f32[16,128,128]{2,1,0:T(8,128)} %bitcast.40), calls=%async_computation | async-start | bytes 2097152 | tf_op jit(solution)/shard_map/all_to_all | solution.py:394
  49.9 28.2 %collective-permute-start.2 = (f32[512,512]{1,0:T(8,128)S(1)}, f32[512,512]{1,0:T(8,128)}, u32[]{:S(2)}, u32[]{:S(2)}) collective-permute-start(f32[512,512]{1,0:T(8,128)S(1)} %copy-done.5), channel_id=1, source_target_pairs={{0,1},{1,0},{2,3},{3,2},{4,5},{5,4},{6,7},{7,6},{8,9},{9,8},{10,11... | collective-permute-start | bytes 3145736 | tf_op jit(solution)/shard_map/ppermute | solution.py:372
  65.8 12.2 %collective-permute-start.5 = (f32[128,128]{1,0:T(8,128)S(1)}, f32[128,128]{1,0:T(8,128)S(1)}, u32[]{:S(2)}, u32[]{:S(2)}) collective-permute-start(f32[128,128]{1,0:T(8,128)S(1)} %reduce_sum.47), channel_id=1, source_target_pairs={{0,1},{1,0},{2,3},{3,2},{4,5},{5,4},{6,7},{7,6},{8,9},{9,8},{10,11... | collective-permute-start | bytes 196616 | tf_op jit(solution)/shard_map/ppermute | solution.py:401
  70.0 37.3 %collective-permute-start.6 = (f32[512,512]{1,0:T(8,128)S(1)}, f32[512,512]{1,0:T(8,128)}, u32[]{:S(2)}, u32[]{:S(2)}) collective-permute-start(f32[512,512]{1,0:T(8,128)S(1)} %get-tuple-element.30.refs_1_.refs_0_), channel_id=1, source_target_pairs={{1,3},{3,5},{5,7},{7,9},{9,11},{11,13},{13,15},{15,17},{17,19},{19... | collective-permute-start | bytes 3145736 | tf_op jit(solution)/shard_map/ppermute | solution.py:373
  72.4 39.0 %collective-permute-start.8 = (f32[512,512]{1,0:T(8,128)}, f32[512,512]{1,0:T(8,128)}, u32[]{:S(2)}, u32[]{:S(2)}) collective-permute-start(f32[512,512]{1,0:T(8,128)} %collective-permute-done.4.refs_1_), channel_id=1, source_target_pairs={{0,2},{2,4},{4,6},{6,8},{8,10},{10,12},{12,14},{14,16},{16,18},{18... | collective-permute-start | bytes 3145736 | tf_op jit(solution)/shard_map/ppermute | solution.py:397
  77.9 33.5 %collective-permute-start.7 = (f32[512,512]{1,0:T(8,128)}, f32[512,512]{1,0:T(8,128)}, u32[]{:S(2)}, u32[]{:S(2)}) collective-permute-start(f32[512,512]{1,0:T(8,128)} %copy-done.12), channel_id=1, source_target_pairs={{0,1},{1,0},{2,3},{3,2},{4,5},{5,4},{6,7},{7,6},{8,9},{9,8},{10,11... | collective-permute-start | bytes 3145736 | tf_op jit(solution)/shard_map/ppermute | solution.py:402
  78.1 13.6 %copy-start.15 = (f32[64,256]{1,0:T(8,128)S(1)}, f32[64,256]{1,0:T(8,128)}, u32[]{:S(2)}) copy-start(f32[64,256]{1,0:T(8,128)} %get-tuple-element.38) | copy-start | bytes 196612
  79.2 12.6 %copy-start.17 = (f32[64,256]{1,0:T(8,128)S(1)}, f32[64,256]{1,0:T(8,128)}, u32[]{:S(2)}) copy-start(f32[64,256]{1,0:T(8,128)} %copy-done.16) | copy-start | bytes 196612
  79.2 12.6 %copy-start.19 = (f32[64,256]{1,0:T(8,128)S(1)}, f32[64,256]{1,0:T(8,128)}, u32[]{:S(2)}) copy-start(f32[64,256]{1,0:T(8,128)} %copy-done.18) | copy-start | bytes 196612
  79.2 39.4 %all-to-all-start.1 = ((f32[16,128,128]{2,1,0:T(8,128)}), f32[16,128,128]{2,1,0:T(8,128)S(1)}, u32[]{:S(2)}, u32[]{:S(2)}) async-start(f32[16,128,128]{2,1,0:T(8,128)} %broadcast_in_dim.33), calls=%async_computation.1 | async-start | bytes 2097152 | tf_op jit(solution)/shard_map/all_to_all | solution.py:404
  85.4 9.9 %copy-start.33 = (f32[128]{0:T(128)S(1)}, f32[128]{0:T(128)}, u32[]{:S(2)}) copy-start(f32[128]{0:T(128)} %param.16) | copy-start | bytes 1540
  118.6 19.4 %copy-start.25 = (f32[4,5,256]{2,0,1:T(4,128)S(1)}, f32[4,5,256]{2,0,1:T(4,128)}, u32[]{:S(2)}) copy-start(f32[4,5,256]{2,0,1:T(4,128)} %get-tuple-element.47) | copy-start | bytes 61444
  121.8 6.5 %collective-permute-start.10 = (f32[640,128]{1,0:T(8,128)S(1)}, f32[640,128]{1,0:T(8,128)}, u32[]{:S(2)}, u32[]{:S(2)}) collective-permute-start(f32[640,128]{1,0:T(8,128)S(1)} %pad_maximum_fusion.1), channel_id=1, source_target_pairs={{0,32},{32,0},{64,96},{96,64},{128,160},{160,128},{192,224},{224,1... | collective-permute-start | bytes 983048 | tf_op jit(solution)/shard_map/ppermute | solution.py:419
  121.9 31.4 %collective-permute-start.9 = (f32[512,512]{1,0:T(8,128)}, f32[512,512]{1,0:T(8,128)}, u32[]{:S(2)}, u32[]{:S(2)}) collective-permute-start(f32[512,512]{1,0:T(8,128)} %collective-permute-done.2.refs_1_), channel_id=1, source_target_pairs={{0,2},{2,4},{4,6},{6,8},{8,10},{10,12},{12,14},{14,16},{16,18},{18... | collective-permute-start | bytes 3145736 | tf_op jit(solution)/shard_map/ppermute | solution.py:413
  129.4 5.3 %collective-permute-start.11 = (f32[128,128]{1,0:T(8,128)S(1)}, f32[128,128]{1,0:T(8,128)S(1)}, u32[]{:S(2)}, u32[]{:S(2)}) collective-permute-start(f32[128,128]{1,0:T(8,128)S(1)} %slice.98), channel_id=1, source_target_pairs={{0,64},{32,96},{64,0},{96,32},{128,192},{160,224},{192,128},{224,1... | collective-permute-start | bytes 196616 | tf_op jit(solution)/shard_map/ppermute | solution.py:421
  130.2 21.4 %collective-permute-start.14 = (f32[512,128]{1,0:T(8,128)}, f32[512,128]{1,0:T(8,128)}, u32[]{:S(2)}, u32[]{:S(2)}) collective-permute-start(f32[512,128]{1,0:T(8,128)} %slice_select_fusion), channel_id=1, source_target_pairs={{0,128},{32,160},{1,129},{33,161},{2,130},{34,162},{3,131},{35,163... | collective-permute-start | bytes 786440 | tf_op jit(solution)/shard_map/ppermute | solution.py:432
  131.6 20.4 %collective-permute-start.15 = (f32[512,128]{1,0:T(8,128)}, f32[512,128]{1,0:T(8,128)}, u32[]{:S(2)}, u32[]{:S(2)}) collective-permute-start(f32[512,128]{1,0:T(8,128)} %slice_select_fusion), channel_id=1, source_target_pairs={{0,192},{32,224},{1,193},{33,225},{2,194},{34,226},{3,195},{35,227... | collective-permute-start | bytes 786440 | tf_op jit(solution)/shard_map/ppermute | solution.py:432
  132.9 19.1 %collective-permute-start.13 = (f32[512,128]{1,0:T(8,128)}, f32[512,128]{1,0:T(8,128)}, u32[]{:S(2)}, u32[]{:S(2)}) collective-permute-start(f32[512,128]{1,0:T(8,128)} %slice_select_fusion), channel_id=1, source_target_pairs={{0,64},{32,96},{1,65},{33,97},{2,66},{34,98},{3,67},{35,99},{4,68}... | collective-permute-start | bytes 786440 | tf_op jit(solution)/shard_map/ppermute | solution.py:432
  135.3 14.7 %collective-permute-start.12 = (f32[128,128]{1,0:T(8,128)}, f32[128,128]{1,0:T(8,128)}, u32[]{:S(2)}, u32[]{:S(2)}) collective-permute-start(f32[128,128]{1,0:T(8,128)} %slice_add_fusion), channel_id=1, source_target_pairs={{0,128},{32,160},{64,192},{96,224},{128,0},{160,32},{192,64},{224,... | collective-permute-start | bytes 196616 | tf_op jit(solution)/shard_map/ppermute | solution.py:422
  150.0 25.5 %copy-start.11 = (f32[512,512]{1,0:T(8,128)S(1)}, f32[512,512]{1,0:T(8,128)}, u32[]{:S(2)}) copy-start(f32[512,512]{1,0:T(8,128)} %copy-done.10) | copy-start | bytes 3145732
  153.2 32.3 %collective-permute-start.16 = (f32[512,512]{1,0:T(8,128)}, f32[512,512]{1,0:T(8,128)}, u32[]{:S(2)}, u32[]{:S(2)}) collective-permute-start(f32[512,512]{1,0:T(8,128)} %column_step_others.3), channel_id=1, source_target_pairs={{0,1},{1,0},{2,3},{3,2},{4,5},{5,4},{6,7},{7,6},{8,9},{9,8},{10,11... | collective-permute-start | bytes 3145736 | tf_op jit(solution)/shard_map/ppermute | solution.py:439
  180.6 4.9 %copy-start.3 = (f32[512,512]{1,0:T(8,128)S(1)}, f32[512,512]{1,0:T(8,128)}, u32[]{:S(2)}) copy-start(f32[512,512]{1,0:T(8,128)} %copy-done.2) | copy-start | bytes 3145732
  (21 other events, 36.2 us)
